TPU v7x, 32 devices: a whole 2x2x4 slice. The times are simulated.
32 devices in a mesh: groups: 2 (over y), seq: 16 (over z, x, core).
Axes of the slice: x: 2, y: 2, z: 4, core: 2. Of those that a mesh axis runs over, the one named last changes fastest.
Arguments:
- token_ids: int32 [4096], P('groups'), parts along dimension 0, may hold values from 0 to 511
- vocab_table: bfloat16 [512, 3, 4096], P(None, None, 'seq'), may hold values from -6 to 6
- short_filter: float32 [7, 3, 4096], replicated, may hold values from -2 to 2
- residue: float32 [4096, 16], replicated, may hold values from -1.5 to 1.5
- decay: float32 [4096, 16], replicated, may hold values from 0.2 to 64
- skip_gain: float32 [4096], replicated, may hold values from -3 to 3
Outputs:
- hyena_out: bfloat16 [4096, 4096], P(('groups', 'seq')), parts along dimension 0
There are 2 independent parts, one for each index of `groups`. A program takes and returns all parts, laid end to end along the dimension named above; an argument that names none is the same for every part. Nothing has to cross between parts.
All inputs are finite; a program needn't handle non-finite values.
Results may differ from a plain program's by a relative error of at most 0.012.
Values may be sent and summed in bfloat16 or wider, within the bound.
A program may use at most 192 MiB of HBM per device.

v0:
```python
import math

import jax
import jax.numpy as jnp
from jax import lax
from jax.sharding import PartitionSpec as P

HIGHEST = lax.Precision.HIGHEST


def angle_tables(first_index, second_index, modulus):
    product = first_index[:, None] * second_index[None, :] % modulus
    angle = product.astype(jnp.float32) * (2.0 * math.pi / modulus)
    return (jnp.cos(angle), jnp.sin(angle))


def short_conv(padded, taps, count):
    width = taps.shape[0]
    total = jnp.zeros((count,) + padded.shape[1:], jnp.float32)
    for lag in range(width):
        start = width - 1 - lag
        total = total + taps[lag] * padded[start : start + count].astype(jnp.float32)
    return total


def filter_spectrum(freq, total, pole, gap, tail, scale):
    theta = freq.astype(jnp.float32) * (2.0 * math.pi / total)
    sine = jnp.sin(theta)[:, :, None, None]
    halfsq = (jnp.sin(0.5 * theta) ** 2)[:, :, None, None]
    parity = (1 - 2 * (freq % 2)).astype(jnp.float32)[:, :, None, None]
    shape_out = freq.shape + (pole.shape[0],)
    real_part = jnp.zeros(shape_out, jnp.float32)
    imag_part = jnp.zeros(shape_out, jnp.float32)
    for first in range(0, pole.shape[1], 4):
        part_pole = pole[:, first : first + 4]
        dreal = gap[:, first : first + 4] + 2.0 * part_pole * halfsq
        dimag = part_pole * sine
        factor = (
            scale[:, first : first + 4]
            * (1.0 - tail[:, first : first + 4] * parity)
            / (dreal * dreal + dimag * dimag)
        )
        real_part = real_part + jnp.sum(factor * dreal, axis=-1)
        imag_part = imag_part - jnp.sum(factor * dimag, axis=-1)
    return (real_part, imag_part)


def convolve(gated, skip, filters, total, move_forward, move_back):
    pieces, block, width = gated.shape
    span = 2 * pieces
    outer_index = jnp.arange(span, dtype=jnp.int32)
    piece_index = jnp.arange(pieces, dtype=jnp.int32)
    outer_cos, outer_sin = angle_tables(outer_index, piece_index, span)
    real_part = jnp.einsum("kp,ptc->ktc", outer_cos, gated, precision=HIGHEST)
    imag_part = -jnp.einsum("kp,ptc->ktc", outer_sin, gated, precision=HIGHEST)
    times = jnp.arange(block, dtype=jnp.int32)
    twist_cos, twist_sin = angle_tables(outer_index, times, total)
    twist_cos = twist_cos[:, :, None]
    twist_sin = twist_sin[:, :, None]
    turned_real = twist_cos * real_part + twist_sin * imag_part
    turned_imag = twist_cos * imag_part - twist_sin * real_part
    moved = move_forward(jnp.stack([turned_real, turned_imag]))
    count = moved.shape[1]
    length = moved.shape[2]
    positions = jnp.arange(length, dtype=jnp.int32)
    inner_cos, inner_sin = angle_tables(positions, positions, length)
    freq_real = jnp.einsum("mt,ktc->kmc", inner_cos, moved[0], precision=HIGHEST) + jnp.einsum(
        "mt,ktc->kmc", inner_sin, moved[1], precision=HIGHEST
    )
    freq_imag = jnp.einsum("mt,ktc->kmc", inner_cos, moved[1], precision=HIGHEST) - jnp.einsum(
        "mt,ktc->kmc", inner_sin, moved[0], precision=HIGHEST
    )
    owned = jnp.arange(count, dtype=jnp.int32)
    freq = (owned[:, None] + span * positions[None, :]) % total
    filt_real, filt_imag = filter_spectrum(freq, total, *filters)
    prod_real = freq_real * filt_real - freq_imag * filt_imag
    prod_imag = freq_real * filt_imag + freq_imag * filt_real
    back_real = jnp.einsum("mt,kmc->ktc", inner_cos, prod_real, precision=HIGHEST) - jnp.einsum(
        "mt,kmc->ktc", inner_sin, prod_imag, precision=HIGHEST
    )
    back_imag = jnp.einsum("mt,kmc->ktc", inner_cos, prod_imag, precision=HIGHEST) + jnp.einsum(
        "mt,kmc->ktc", inner_sin, prod_real, precision=HIGHEST
    )
    undo_cos, undo_sin = angle_tables(owned, positions, total)
    undo_cos = undo_cos[:, :, None]
    undo_sin = undo_sin[:, :, None]
    untwist_real = undo_cos * back_real - undo_sin * back_imag
    untwist_imag = undo_cos * back_imag + undo_sin * back_real
    returned = move_back(jnp.stack([untwist_real, untwist_imag]))
    last_cos, last_sin = angle_tables(piece_index, outer_index, span)
    convolved = (
        jnp.einsum("pk,ktc->ptc", last_cos, returned[0], precision=HIGHEST)
        - jnp.einsum("pk,ktc->ptc", last_sin, returned[1], precision=HIGHEST)
    ) * (1.0 / total)
    return convolved + skip * gated


def unchanged(value):
    return value


def body(token_ids, vocab_table, short_filter, residue, decay, skip_gain):
    pieces = lax.axis_size("seq")
    place = lax.axis_index("seq")
    length = token_ids.shape[0]
    local = length // pieces
    share = vocab_table.shape[2]
    rim = short_filter.shape[0] - 1
    total = 2 * length
    rate = decay / length
    pole = jnp.exp(-rate)
    gap = -jnp.expm1(-rate)
    tail = jnp.exp(-decay)
    scale = residue * jnp.sqrt(2.0 * rate)
    first_channel = place * share
    chan_taps = lax.dynamic_slice_in_dim(short_filter, first_channel, share, 2)
    chan_filters = (
        lax.dynamic_slice_in_dim(pole, first_channel, share, 0),
        lax.dynamic_slice_in_dim(gap, first_channel, share, 0),
        lax.dynamic_slice_in_dim(tail, first_channel, share, 0),
        lax.dynamic_slice_in_dim(scale, first_channel, share, 0),
    )
    chan_skip = lax.dynamic_slice_in_dim(skip_gain, first_channel, share, 0)
    streams = jnp.take(vocab_table, token_ids, axis=0)
    padded = jnp.pad(streams, ((rim, 0), (0, 0), (0, 0)))
    mixed = short_conv(padded, chan_taps, length)
    query = mixed[:, 0]
    gated = (mixed[:, 1] * mixed[:, 2]).reshape(pieces, local, share)
    convolved = convolve(gated, chan_skip, chan_filters, total, unchanged, unchanged)
    output = (query * convolved.reshape(length, share)).astype(jnp.bfloat16)
    return lax.all_to_all(output, "seq", split_axis=0, concat_axis=1, tiled=True)


def solution(mesh):
    placed = (P("groups"), P(None, None, "seq"), P(), P(), P(), P())
    return jax.shard_map(
        body, mesh=mesh, in_specs=placed, out_specs=P(("groups", "seq"), None), check_vma=False
    )
```

profile of v0, /device:TPU:0, one launch (start us, length us, event | category | flops | bytes accessed | tf_op | source)
XLA Modules:
  0.0 295.5 jit_solution(17280626911231516608)
XLA Ops:
  0.0 0.0 copy-start
  0.0 0.8 fusion.84
  0.8 0.7 compare_and_fusion
  1.5 0.1 fusion.77
  1.6 0.1 sine_multiply_fusion
  1.8 1.1 constant_dynamic-slice_fusion.5
  2.9 0.0 copy-done
  2.9 23.5 %gather_fusion = bf16[2048,3,256]{2,0,1:T(8,128)(2,1)} fusion(bf16[512,3,256]{2,0,1:T(8,128)(2,1)S(1)} %copy-done, s32[2048]{0:T(1024)S(1)} %fusion.84), kind=kCustom, calls=%fused_computation | custom fusion | bytes 6299648 | tf_op jit(solution)/shard_map/jit(_take)/gather | solution.py:124
  26.4 2.1 broadcast_select_fusion
  28.6 5.6 %multiply_add_fusion.4 = f32[2048,3,256]{2,0,1:T(8,128)S(1)} fusion(bf16[2048,3,256]{2,0,1:T(8,128)(2,1)S(1)} %broadcast_select_fusion, f32[3,256]{1,0:T(4,128)S(1)} %get-tuple-element.62, f32[3,256]{1,0:T(4,128)S(1)} %get-tuple-element.63, f32[3,256]{1,0:T(4,128)S(1)} %get-tuple-element.64, f32[3,256]{1,0:T(4,128)S(1)} %get-tuple-element.65, ...), kind=kLoop, calls=%fused_computation.29 | loop fusion | flops 31457280 | bytes 9458688 | tf_op jit(solution)/shard_map/add | solution.py:22
  34.2 1.7 slice_multiply_fusion
  35.9 0.0 copy-start.4
  35.9 5.6 %fusion.15 = f32[32,128,256]{2,0,1:T(8,128)} fusion(f32[16,128,256]{2,1,0:T(8,128)S(1)} %bitcast.84), kind=kOutput, calls=%fused_computation.54 | convolution fusion | flops 201333760 | bytes 6291456 | tf_op jit(solution)/shard_map/kp,ptc->ktc/dot_general | solution.py:55
  41.5 0.1 copy.173
  41.6 0.1 copy.175
  41.7 9.1 %multiply_add_fusion.5 = (f32[32,128,256]{2,0,1:T(8,128)}, f32[32,128,256]{2,0,1:T(8,128)}) fusion(f32[32,128,256]{2,0,1:T(8,128)} %fusion.15, f32[32,128]{0,1:T(8,128)S(1)} %copy.175, f32[32,128]{0,1:T(8,128)S(1)} %copy.173, f32[16,128,256]{2,1,0:T(8,128)S(1)} %bitcast.85), kind=kOutput, calls=%fused_computation.41 | convolution fusion | flops 208673792 | bytes 14712832 | tf_op jit(solution)/shard_map/kp,ptc->ktc/dot_general | solution.py:54
  50.8 0.0 copy-done.4
  50.8 5.3 %copy.177 = f32[32,128,256]{1,2,0:T(8,128)} copy(f32[32,128,256]{2,0,1:T(8,128)} %get-tuple-element.20) | data formatting | bytes 8388608 | tf_op jit(solution)/shard_map/add | solution.py:60
  56.1 7.0 %fusion.32 = f32[32,256,128]{2,1,0:T(8,128)} fusion(f32[32,128,256]{1,2,0:T(8,128)} %copy.177), kind=kOutput, calls=%fused_computation.75 | convolution fusion | flops 1610842112 | bytes 8388608 | tf_op jit(solution)/shard_map/mt,ktc->kmc/dot_general | solution.py:67
  63.1 5.3 %copy.178 = f32[32,128,256]{1,2,0:T(8,128)} copy(f32[32,128,256]{2,0,1:T(8,128)} %get-tuple-element.21) | data formatting | bytes 8388608 | tf_op jit(solution)/shard_map/sub | solution.py:61
  68.4 0.0 copy-start.2
  68.4 0.0 copy-start.6
  68.4 18.2 %fusion.30 = f32[32,256,128]{2,1,0:T(8,128)} fusion(f32[32,128,256]{1,2,0:T(8,128)} %copy.178), kind=kOutput, calls=%fused_computation.73 | convolution fusion | flops 1610842112 | bytes 8388608 | tf_op jit(solution)/shard_map/mt,ktc->kmc/dot_general | solution.py:70
  86.6 0.0 copy-done.2
  86.6 0.0 copy-done.6
  86.6 0.0 copy-start.7
  86.6 5.5 %convolution_add_fusion.1 = f32[32,256,128]{2,1,0:T(8,128)} fusion(f32[32,256,128]{2,1,0:T(8,128)S(1)} %copy-done.6, f32[32,128,256]{1,2,0:T(8,128)S(1)} %copy-done.2), kind=kOutput, calls=%fused_computation.50 | convolution fusion | flops 1611890688 | bytes 12582912 | tf_op jit(solution)/shard_map/mt,ktc->kmc/dot_general | solution.py:67
  92.1 0.0 copy-done.7
  92.1 0.7 dynamic-slice_multiply_fusion
  93.0 38.2 %fusion.2 = (f32[32,128,256]{2,1,0:T(8,128)}, f32[32,128,256]{2,1,0:T(8,128)}, f32[32,128,256]{2,1,0:T(8,128)}, f32[32,128,256]{2,1,0:T(8,128)}, f32[32,128,256]{2,1,0:T(8,128)}, /*index=5*/f32[32,128,256]{2,1,0:T(8,128)}) fusion(f32[32,128]{1,0:T(8,128)S(1)} %get-tuple-element.58, f32[256,4]{0,1:T(4,128)S(1)} %get-tuple-element.55, ...), kind=kLoop, calls=%fused_computation.11 | loop fusion | flops 169869312 | bytes 25276416 | tf_op jit(solution)/shard_map/reduce_sum | solution.py:44
  131.1 5.6 %copy.179 = f32[32,128,256]{1,2,0:T(8,128)} copy(f32[32,128,256]{2,1,0:T(8,128)} %get-tuple-element.6) | data formatting | bytes 8388608 | tf_op jit(solution)/shard_map/reduce_sum | solution.py:43
  136.7 5.6 %copy.181 = f32[32,128,256]{1,2,0:T(8,128)} copy(f32[32,128,256]{2,1,0:T(8,128)} %get-tuple-element.15) | data formatting | bytes 8388608 | tf_op jit(solution)/shard_map/reduce_sum | solution.py:43
  142.3 5.6 %copy.182 = f32[32,128,256]{1,2,0:T(8,128)} copy(f32[32,128,256]{2,1,0:T(8,128)} %get-tuple-element.13) | data formatting | bytes 8388608 | tf_op jit(solution)/shard_map/reduce_sum | solution.py:43
  147.8 5.6 %copy.185 = f32[32,128,256]{1,2,0:T(8,128)} copy(f32[32,128,256]{2,1,0:T(8,128)} %get-tuple-element.5) | data formatting | bytes 8388608 | tf_op jit(solution)/shard_map/reduce_sum | solution.py:44
  153.4 5.6 %copy.187 = f32[32,128,256]{1,2,0:T(8,128)} copy(f32[32,128,256]{2,1,0:T(8,128)} %get-tuple-element.16) | data formatting | bytes 8388608 | tf_op jit(solution)/shard_map/reduce_sum | solution.py:44
  159.0 5.6 %copy.188 = f32[32,128,256]{1,2,0:T(8,128)} copy(f32[32,128,256]{2,1,0:T(8,128)} %get-tuple-element.14) | data formatting | bytes 8388608 | tf_op jit(solution)/shard_map/reduce_sum | solution.py:44
  164.6 13.4 %fusion.5 = (f32[32,128,256]{2,1,0:T(8,128)}, f32[32,128,256]{2,1,0:T(8,128)}) fusion(f32[256,4]{0,1:T(4,128)S(1)} %get-tuple-element.54, f32[32,128]{1,0:T(8,128)S(1)} %get-tuple-element.58, f32[32,128]{1,0:T(8,128)S(1)} %get-tuple-element.57, f32[256,4]{0,1:T(4,128)S(1)} %get-tuple-element.49, f32[256,4]{0,1:T(4,128)S(1)} %get-tuple-element.45, ...), kind=kLoop, calls=%fused_computation.14 | loop fusion | flops 56623104 | bytes 8458240 | tf_op jit(solution)/shard_map/reduce_sum | solution.py:44
  177.9 5.6 %copy.180 = f32[32,128,256]{1,2,0:T(8,128)} copy(f32[32,128,256]{2,1,0:T(8,128)} %get-tuple-element.8) | data formatting | bytes 8388608 | tf_op jit(solution)/shard_map/reduce_sum | solution.py:43
  183.5 5.6 %copy.186 = f32[32,128,256]{1,2,0:T(8,128)} copy(f32[32,128,256]{2,1,0:T(8,128)} %get-tuple-element.7) | data formatting | bytes 8388608 | tf_op jit(solution)/shard_map/reduce_sum | solution.py:44
  189.1 0.0 copy-start.3
  189.1 22.1 %fusion.12 = (f32[32,128,256]{1,2,0:T(8,128)S(1)}, f32[32,128,256]{1,2,0:T(8,128)}, f32[32,128,256]{1,2,0:T(8,128)}, f32[32,256,128]{2,1,0:T(8,128)}) fusion(f32[32,256,128]{2,1,0:T(8,128)} %convolution_add_fusion.1, f32[32,128,256]{1,2,0:T(8,128)} %copy.188, f32[32,128,256]{1,2,0:T(8,128)} %copy.187, f32[32,128,256]{1,2,0:T(8,128)} %copy.186, ...), kind=kOutput, calls=%fused_computation.32 | convolution fusion | flops 1622376448 | bytes 62914560 | tf_op jit(solution)/shard_map/mt,ktc->kmc/dot_general | solution.py:70
  211.2 0.0 copy-done.3
  211.2 6.3 %fusion.13 = f32[32,128,256]{1,2,0:T(8,128)S(1)} fusion(f32[32,128,256]{1,2,0:T(8,128)} %get-tuple-element.19, f32[32,256,128]{2,1,0:T(8,128)} %get-tuple-element.59, f32[32,128,256]{1,2,0:T(8,128)} %get-tuple-element.18, f32[32,256,128]{2,1,0:T(8,128)S(1)} %copy-done.3), kind=kLoop, calls=%fused_computation.33 | loop fusion | flops 3145728 | bytes 20971520 | tf_op jit(solution)/shard_map/add | solution.py:77
  217.5 3.8 %fusion.26 = f32[32,256,128]{2,1,0:T(8,128)S(1)} fusion(f32[32,128,256]{1,2,0:T(8,128)S(1)} %fusion.13), kind=kOutput, calls=%fused_computation.69 | convolution fusion | flops 1610842112 | bytes 8388608 | tf_op jit(solution)/shard_map/mt,kmc->ktc/dot_general | solution.py:81
  221.3 3.8 %fusion.28 = f32[32,256,128]{2,1,0:T(8,128)S(1)} fusion(f32[32,128,256]{1,2,0:T(8,128)S(1)} %get-tuple-element.17), kind=kOutput, calls=%fused_computation.71 | convolution fusion | flops 1610842112 | bytes 8388608 | tf_op jit(solution)/shard_map/mt,kmc->ktc/dot_general | solution.py:78
  225.1 4.0 %convolution_add_fusion = f32[32,256,128]{2,1,0:T(8,128)S(1)} fusion(f32[32,256,128]{2,1,0:T(8,128)S(1)} %fusion.26, f32[32,128,256]{1,2,0:T(8,128)S(1)} %get-tuple-element.17), kind=kOutput, calls=%fused_computation.47 | convolution fusion | flops 1611890688 | bytes 12582912 | tf_op jit(solution)/shard_map/mt,kmc->ktc/dot_general | solution.py:81
  229.1 6.7 %add_bitcast_fusion = (f32[32,128,256]{1,2,0:T(8,128)}, f32[32,128,256]{1,2,0:T(8,128)}) fusion(f32[32,256,128]{2,1,0:T(8,128)S(1)} %convolution_add_fusion, f32[32,128]{1,0:T(8,128)S(1)} %get-tuple-element.68, f32[32,128]{1,0:T(8,128)S(1)} %get-tuple-element.69, f32[32,256,128]{2,1,0:T(8,128)S(1)} %fusion.28, f32[32,128,256]{1,2,0:T(8,128)S(1)} %fusion.13), kind=kOutput, calls=%fused_computation.36 | convolution fusion | flops 1618182144 | bytes 21004288 | tf_op jit(solution)/shard_map/mt,kmc->ktc/dot_general | solution.py:78
  235.7 5.5 %copy.189 = f32[32,128,256]{2,0,1:T(8,128)} copy(f32[32,128,256]{1,2,0:T(8,128)} %get-tuple-element.23) | data formatting | bytes 8388608 | tf_op jit(solution)/shard_map/sub | solution.py:87
  241.2 5.6 %fusion.70 = f32[16,128,256]{2,0,1:T(8,128)} fusion(f32[32,128,256]{2,0,1:T(8,128)} %copy.189), kind=kOutput, calls=%fused_computation.127 | convolution fusion | flops 201333760 | bytes 6291456 | tf_op jit(solution)/shard_map/pk,ktc->ptc/dot_general | solution.py:92
  246.9 0.0 copy-start.5
  246.9 5.6 %copy.190 = f32[32,128,256]{2,0,1:T(8,128)} copy(f32[32,128,256]{1,2,0:T(8,128)} %get-tuple-element.22) | data formatting | bytes 8388608 | tf_op jit(solution)/shard_map/add | solution.py:88
  252.5 0.8 dynamic_slice.23
  253.3 0.0 copy-done.5
  253.3 0.0 copy-start.1
  253.3 7.8 %fusion.14 = bf16[16,128,256]{2,0,1:T(8,128)(2,1)S(1)} fusion(f32[16,128,256]{2,1,0:T(8,128)} %bitcast.87, f32[16,128,256]{2,0,1:T(8,128)} %fusion.70, f32[16,128,256]{2,1,0:T(8,128)S(1)} %bitcast.86, f32[32,128,256]{2,0,1:T(8,128)} %copy.190, f32[256]{0:T(256)S(1)} %dynamic_slice.23), kind=kOutput, calls=%fused_computation.53 | convolution fusion | flops 204479488 | bytes 11535360 | tf_op jit(solution)/shard_map/pk,ktc->ptc/dot_general | solution.py:93
  261.1 0.3 copy.193
  261.4 31.9 %all_to_all.16 = bf16[16,128,256]{2,1,0:T(8,128)(2,1)S(1)} all-to-all(bf16[16,128,256]{2,1,0:T(8,128)(2,1)S(1)} %copy.193), channel_id=1, replica_groups=mesh['groups'=2,'seq'=16] {'seq'}, dimensions={0} | all-to-all | bytes 2097152 | tf_op jit(solution)/shard_map/all_to_all | solution.py:131
  293.3 0.7 copy.194
  294.0 1.3 copy.195
  295.3 0.0 copy-done.1
  (11 shorter events, 0.1 us)
Async XLA Ops:
  0.0 2.9 copy-start
  35.9 14.9 %copy-start.4 = (f32[2048,1,256]{2,0,1:T(8,128)}, f32[2048,1,256]{2,0,1:T(8,128)S(1)}, u32[]{:S(2)}) copy-start(f32[2048,1,256]{2,0,1:T(8,128)S(1)} %get-tuple-element.24) | copy-start | bytes 6291460
  68.4 18.2 %copy-start.2 = (f32[32,128,256]{1,2,0:T(8,128)S(1)}, f32[32,128,256]{1,2,0:T(8,128)}, u32[]{:S(2)}) copy-start(f32[32,128,256]{1,2,0:T(8,128)} %copy.178) | copy-start | bytes 12582916
  68.4 18.2 %copy-start.6 = (f32[32,256,128]{2,1,0:T(8,128)S(1)}, f32[32,256,128]{2,1,0:T(8,128)}, u32[]{:S(2)}) copy-start(f32[32,256,128]{2,1,0:T(8,128)} %fusion.32) | copy-start | bytes 12582916
  86.6 5.5 %copy-start.7 = (f32[4096,16]{0,1:T(8,128)S(1)}, f32[4096,16]{0,1:T(8,128)}, u32[]{:S(2)}) copy-start(f32[4096,16]{0,1:T(8,128)} %param.10) | copy-start | bytes 786436
  189.1 22.1 %copy-start.3 = (f32[32,256,128]{2,1,0:T(8,128)S(1)}, f32[32,256,128]{2,1,0:T(8,128)}, u32[]{:S(2)}) copy-start(f32[32,256,128]{2,1,0:T(8,128)} %convolution_add_fusion.1) | copy-start | bytes 12582916
  246.9 6.4 %copy-start.5 = (f32[2048,1,256]{2,0,1:T(8,128)S(1)}, f32[2048,1,256]{2,0,1:T(8,128)}, u32[]{:S(2)}) copy-start(f32[2048,1,256]{2,0,1:T(8,128)} %copy-done.4) | copy-start | bytes 6291460
  253.3 42.0 %copy-start.1 = (bf16[512,3,256]{2,0,1:T(8,128)(2,1)S(1)}, bf16[512,3,256]{2,0,1:T(8,128)(2,1)}, u32[]{:S(2)}) copy-start(bf16[512,3,256]{2,0,1:T(8,128)(2,1)} %param.7) | copy-start | bytes 2359300
where the time goes:
time: 300 us; the launch traced here: 295 us
  matrix products  99.2 us (33%)
  local copies, waits for them, and re-layouts  94.3 us (31%)
  other arithmetic  69.7 us (23%)
  blocking collectives  31.9 us (11%)
    reduce_sum x2, other arithmetic, filter_spectrum(): imag_part = imag_part - jnp.sum(factor * dimag, axis=-1)  51.5 us
    all_to_all x1, blocking collectives, body(): lax.all_to_all(output, 'seq', split_axis=0, concat_axis=1, tiled=True)  31.9 us
    gather x1, local copies, waits for them, and re-layouts, body(): streams = jnp.take(vocab_table, token_ids, axis=0)  23.5 us
    reduce_sum x4, local copies, waits for them, and re-layouts, filter_spectrum(): real_part = real_part + jnp.sum(factor * dreal, axis=-1)  22.3 us
    reduce_sum x4, local copies, waits for them, and re-layouts, filter_spectrum(): imag_part = imag_part - jnp.sum(factor * dimag, axis=-1)  22.3 us
    dot_general x1, matrix products, convolve(): jnp.einsum('mt,ktc->kmc', inner_sin, moved[0], precision=HIGHEST)  22.1 us
    dot_general x1, matrix products, convolve(): jnp.einsum('mt,ktc->kmc', inner_cos, moved[1], precision=HIGHEST)  18.2 us
    dot_general x1, matrix products, convolve(): real_part = jnp.einsum('kp,ptc->ktc', outer_cos, gated, precision=HIGHEST)  9.14 us

commit v1 on v0

--- a/solution.py
+++ b/solution.py
@@ -1,8 +1,11 @@
+import functools
 import math
 
 import jax
 import jax.numpy as jnp
 from jax import lax
+from jax.experimental import pallas as pl
+from jax.experimental.pallas import tpu as pltpu
 from jax.sharding import PartitionSpec as P
 
 HIGHEST = lax.Precision.HIGHEST
@@ -131,8 +134,258 @@
     return lax.all_to_all(output, "seq", split_axis=0, concat_axis=1, tiled=True)
 
 
+LANES = 128
+SUB = 8
+HALO = 8
+UNROLL = 8
+MESH = pl.DeviceIdType.MESH
+
+
+def wide(row):
+    return jnp.broadcast_to(row, (SUB, LANES))
+
+
+def scan_kernel(
+    pieces,
+    local,
+    width,
+    modes,
+    ids_ref,
+    tab_ref,
+    taps_ref,
+    decay_ref,
+    residue_ref,
+    skip_ref,
+    out_ref,
+    hot_ref,
+    x_ref,
+    query_ref,
+    gated_ref,
+    end_ref,
+    begin_ref,
+    coef_ref,
+    turn_ref,
+    send_ref,
+    send_sem,
+    recv_sem,
+    own_sem,
+):
+    me = lax.axis_index("seq")
+    half = pieces // 2
+    near = me // half
+    slots = pieces // SUB
+    parts = half // SUB
+    share = skip_ref.shape[1]
+    vocab = tab_ref.shape[0]
+    blocks = share // LANES
+    length = pieces * local
+    barrier = pltpu.get_barrier_semaphore()
+    for step in range(1, pieces):
+        peer = lax.rem(me + step, pieces)
+        pl.semaphore_signal(barrier, inc=1, device_id={"seq": peer}, device_id_type=MESH)
+
+    rows = (HALO + local) * pieces
+    cut = rows // 4
+    for i in range(4):
+        span = pl.ds(i * cut, cut)
+        entry = lax.broadcasted_iota(jnp.int32, (cut, vocab), 1)
+        hot_ref[span, :] = jnp.where(ids_ref[span, :] == entry, 1.0, 0.0).astype(jnp.bfloat16)
+
+    def remote(block, peer, source):
+        column = pl.ds(pl.multiple_of(source * share + block * LANES, LANES), LANES)
+        return pltpu.make_async_remote_copy(
+            src_ref=send_ref.at[block, peer],
+            dst_ref=out_ref.at[:, column],
+            send_sem=send_sem.at[block, peer],
+            recv_sem=recv_sem.at[block, source],
+            device_id={"seq": peer},
+            device_id_type=MESH,
+        )
+
+    def own(block):
+        column = pl.ds(pl.multiple_of(me * share + block * LANES, LANES), LANES)
+        return pltpu.make_async_copy(send_ref.at[block, me], out_ref.at[:, column], own_sem.at[block])
+
+    for block in range(blocks):
+        lane = pl.ds(block * LANES, LANES)
+        rate = decay_ref[:, lane] / length
+        pole = jnp.exp(-rate)
+        leap = jnp.exp(-rate * local)
+        coef_ref[0] = pole
+        coef_ref[1] = residue_ref[:, lane] * jnp.sqrt(2.0 * rate)
+        skip = wide(skip_ref[:, lane])
+        table = tab_ref[:, block * 3 * LANES : (block + 1) * 3 * LANES]
+        for i in range(4):
+            span = pl.ds(i * cut, cut)
+            x_ref[span, :] = jnp.dot(hot_ref[span, :], table, preferred_element_type=jnp.float32)
+
+        def first_pass(slot, _):
+            base = pl.multiple_of(slot * SUB, SUB)
+            poles = [wide(coef_ref[0, s : s + 1, :]) for s in range(modes)]
+            taps = [
+                [wide(taps_ref[lag, j : j + 1, lane]) for lag in range(width)] for j in range(3)
+            ]
+
+            def step(i, state):
+                state = list(state)
+                mixed = []
+                for j in range(3):
+                    seen = {}
+                    for t in range(1 - width, UNROLL):
+                        at = pl.multiple_of((i * UNROLL + t + HALO) * pieces + base, SUB)
+                        seen[t] = x_ref[pl.ds(at, SUB), j * LANES : (j + 1) * LANES]
+                    totals = []
+                    for t in range(UNROLL):
+                        total = taps[j][0] * seen[t]
+                        for lag in range(1, width):
+                            total = total + taps[j][lag] * seen[t - lag]
+                        totals.append(total)
+                    mixed.append(totals)
+                for t in range(UNROLL):
+                    at = pl.multiple_of((i * UNROLL + t) * pieces + base, SUB)
+                    gated = mixed[1][t] * mixed[2][t]
+                    query_ref[pl.ds(at, SUB), :] = mixed[0][t]
+                    gated_ref[pl.ds(at, SUB), :] = gated
+                    for s in range(modes):
+                        state[s] = poles[s] * state[s] + gated
+                return tuple(state)
+
+            zero = jnp.zeros((SUB, LANES), jnp.float32)
+            state = lax.fori_loop(0, local // UNROLL, step, (zero,) * modes)
+            for s in range(modes):
+                end_ref[pl.ds(pl.multiple_of(s * pieces + base, SUB), SUB), :] = state[s]
+            return 0
+
+        lax.fori_loop(0, slots, first_pass, 0)
+        carry = jnp.zeros((modes, LANES), jnp.float32)
+        for k in range(pieces):
+            begin_ref[pl.ds(k, modes, stride=pieces), :] = carry
+            carry = leap * carry + end_ref[pl.ds(k, modes, stride=pieces), :]
+
+        for side in range(2):
+            group = near if side else 1 - near
+            for part in range(parts):
+                first = group * half + part * SUB
+                base = pl.multiple_of(first, SUB)
+                poles = [wide(coef_ref[0, s : s + 1, :]) for s in range(modes)]
+                coefs = [wide(coef_ref[1, s : s + 1, :]) for s in range(modes)]
+
+                def step(i, state):
+                    state = list(state)
+                    for t in range(UNROLL):
+                        at = pl.multiple_of((i * UNROLL + t) * pieces + base, SUB)
+                        gated = gated_ref[pl.ds(at, SUB), :]
+                        terms = [skip * gated]
+                        for s in range(modes):
+                            state[s] = poles[s] * state[s] + gated
+                            terms.append(coefs[s] * state[s])
+                            if len(terms) == 5:
+                                terms = [((terms[0] + terms[1]) + (terms[2] + terms[3])) + terms[4]]
+                        total = terms[0]
+                        for term in terms[1:]:
+                            total = total + term
+                        turn_ref[pl.ds(pl.multiple_of((i * UNROLL + t) * SUB, SUB), SUB), :] = (
+                            query_ref[pl.ds(at, SUB), :] * total
+                        )
+                    return tuple(state)
+
+                state = tuple(
+                    begin_ref[pl.ds(pl.multiple_of(s * pieces + base, SUB), SUB), :]
+                    for s in range(modes)
+                )
+                lax.fori_loop(0, local // UNROLL, step, state)
+                for k in range(SUB):
+                    send_ref[block, first + k] = turn_ref[pl.ds(k, local, stride=SUB), :].astype(
+                        jnp.bfloat16
+                    )
+                if block == 0 and side == 0 and part == 0:
+                    pl.semaphore_wait(barrier, pieces - 1)
+                for k in range(SUB):
+                    peer = first + lax.rem(me + k, SUB)
+                    if side == 0:
+                        remote(block, peer, me).start()
+                    else:
+
+                        @pl.when(peer != me)
+                        def _():
+                            remote(block, peer, me).start()
+
+                        @pl.when(peer == me)
+                        def _():
+                            own(block).start()
+
+    for block in range(blocks):
+        own(block).wait()
+        for step in range(1, pieces):
+            remote(block, lax.rem(me + step, pieces), me).wait_send()
+        for step in range(1, pieces):
+            remote(block, me, lax.rem(me + step, pieces)).wait_recv()
+
+
+def scan_body(token_ids, vocab_table, short_filter, residue, decay, skip_gain):
+    pieces = lax.axis_size("seq")
+    place = lax.axis_index("seq")
+    length = token_ids.shape[0]
+    local = length // pieces
+    vocab, streams, share = vocab_table.shape
+    width = short_filter.shape[0]
+    modes = decay.shape[1]
+    blocks = share // LANES
+    spread = jnp.concatenate(
+        [
+            jnp.concatenate([jnp.full((1, HALO), -1, jnp.int32), token_ids.reshape(pieces, local)[:-1, local - HALO :]]),
+            token_ids.reshape(pieces, local),
+        ],
+        axis=1,
+    )
+    ids = spread.T.reshape((HALO + local) * pieces, 1)
+    table = vocab_table.reshape(vocab, streams, blocks, LANES).transpose(0, 2, 1, 3)
+    table = table.reshape(vocab, streams * share)
+    start = place * share
+    taps = lax.dynamic_slice_in_dim(short_filter, start, share, 2)
+    chan_decay = lax.dynamic_slice_in_dim(decay, start, share, 0).T
+    chan_residue = lax.dynamic_slice_in_dim(residue, start, share, 0).T
+    skip = lax.dynamic_slice_in_dim(skip_gain, start, share, 0)[None]
+    rows = (HALO + local) * pieces
+    vmem = pl.BlockSpec(memory_space=pltpu.VMEM)
+    return pl.pallas_call(
+        functools.partial(scan_kernel, pieces, local, width, modes),
+        out_shape=jax.ShapeDtypeStruct((local, pieces * share), jnp.bfloat16),
+        in_specs=[vmem] * 6,
+        out_specs=pl.BlockSpec(memory_space=pl.ANY),
+        scratch_shapes=[
+            pltpu.VMEM((rows, vocab), jnp.bfloat16),
+            pltpu.VMEM((rows, streams * LANES), jnp.float32),
+            pltpu.VMEM((length, LANES), jnp.float32),
+            pltpu.VMEM((length, LANES), jnp.float32),
+            pltpu.VMEM((modes * pieces, LANES), jnp.float32),
+            pltpu.VMEM((modes * pieces, LANES), jnp.float32),
+            pltpu.VMEM((2, modes, LANES), jnp.float32),
+            pltpu.VMEM((local * SUB, LANES), jnp.float32),
+            pltpu.VMEM((blocks, pieces, local, LANES), jnp.bfloat16),
+            pltpu.SemaphoreType.DMA((blocks, pieces)),
+            pltpu.SemaphoreType.DMA((blocks, pieces)),
+            pltpu.SemaphoreType.DMA((blocks,)),
+        ],
+        compiler_params=pltpu.CompilerParams(collective_id=0, has_side_effects=True),
+    )(ids, table, taps, chan_decay, chan_residue, skip)
+
+
+def fits(mesh, share, local, width):
+    pieces = mesh.shape["seq"]
+    return share % LANES == 0 and pieces % (2 * SUB) == 0 and local % 16 == 0 and width <= HALO + 1
+
+
 def solution(mesh):
     placed = (P("groups"), P(None, None, "seq"), P(), P(), P(), P())
-    return jax.shard_map(
-        body, mesh=mesh, in_specs=placed, out_specs=P(("groups", "seq"), None), check_vma=False
-    )
+
+    def whole(token_ids, vocab_table, short_filter, residue, decay, skip_gain):
+        pieces = mesh.shape["seq"]
+        local = token_ids.shape[0] // (mesh.shape["groups"] * pieces)
+        share = vocab_table.shape[2] // pieces
+        chosen = scan_body if fits(mesh, share, local, short_filter.shape[0]) else body
+        return jax.shard_map(
+            chosen, mesh=mesh, in_specs=placed, out_specs=P(("groups", "seq"), None), check_vma=False
+        )(token_ids, vocab_table, short_filter, residue, decay, skip_gain)
+
+    return whole

time: 300 us -> 47.9 us (0.16); the launches traced: 295 us -> 47.5 us
  matrix products: 99.2 us -> 0 us
  local copies, waits for them, and re-layouts: 94.3 us -> 10.7 us
  other arithmetic: 69.7 us -> 0.77 us
  Pallas kernels: 0 us -> 36 us
  blocking collectives: 31.9 us -> 0 us
    dot_general x12 -> x0, matrix products: 99.2 us -> none  [the longest x1 22.1 us: convolve(): jnp.einsum('mt,ktc->kmc', inner_sin, moved[0], precision=HIGHEST)]
    reduce_sum x2 -> x0, other arithmetic: 51.5 us -> none  [filter_spectrum(): imag_part = imag_part - jnp.sum(factor * dimag, axis=-1)]
    reduce_sum x8 -> x0, local copies, waits for them, and re-layouts: 44.6 us -> none  [the longest x4 22.3 us: filter_spectrum(): real_part = real_part + jnp.sum(factor * dreal, axis=-1)]
    pallas_call x0 -> x1, Pallas kernels: none -> 36 us  [scan_body(): pl.pallas_call(functools.partial(scan_kernel, pieces, local, width, modes...]
    all_to_all x1 -> x0, blocking collectives: 31.9 us -> none  [body(): lax.all_to_all(output, 'seq', split_axis=0, concat_axis=1, tiled=True)]
    gather x1 -> x0, local copies, waits for them, and re-layouts: 23.5 us -> none  [body(): streams = jnp.take(vocab_table, token_ids, axis=0)]
    add x2 -> x0, other arithmetic: 11.9 us -> none  [the longest x1 6.26 us: convolve(): prod_imag = freq_real * filt_imag + freq_imag * filt_real]
    add x2 -> x0, local copies, waits for them, and re-layouts: 10.9 us -> none  [the longest x1 5.65 us: convolve(): untwist_imag = undo_cos * back_imag + undo_sin * back_real]
where the time goes in v1:
time: 47.9 us; the launch traced here: 47.5 us
  Pallas kernels  36 us (75%)
  local copies, waits for them, and re-layouts  10.7 us (22%)
  other arithmetic  0.77 us (2%)
    pallas_call x1, Pallas kernels, scan_body(): pl.pallas_call(functools.partial(scan_kernel, pieces, local, width, modes...  36 us
    unnamed x5, local copies, waits for them, and re-layouts  4.32 us
    reshape x1, local copies, waits for them, and re-layouts, scan_body(): ids = spread.T.reshape((HALO + local) * pieces, 1)  1.61 us
    dynamic_slice x1, local copies, waits for them, and re-layouts, scan_body(): skip = lax.dynamic_slice_in_dim(skip_gain, start, share, 0)[None]  1.37 us
    transpose x1, local copies, waits for them, and re-layouts, scan_body(): chan_residue = lax.dynamic_slice_in_dim(residue, start, share, 0).T  1.34 us
    reshape x1, local copies, waits for them, and re-layouts, scan_body(): table = table.reshape(vocab, streams * share)  1.16 us

profile of v1, /device:TPU:0, one launch (start us, length us, event | category | flops | bytes accessed | tf_op | source)
XLA Modules:
  0.0 47.5 jit_solution(380830926756088742)
XLA Ops:
  0.0 0.0 copy-start
  0.0 1.4 %dynamic_slice.15 = f32[256]{0:T(256)} dynamic-slice(f32[4096]{0:T(1024)} %param.11, s32[]{:T(128)S(6)} %select_n.2), dynamic_slice_sizes={256} | dynamic-slice | bytes 2052 | tf_op jit(solution)/shard_map/dynamic_slice | solution.py:348
  1.4 0.8 %slice.4 = s32[15,8]{1,0:T(8,128)S(1)} slice(s32[16,128]{1,0:T(8,128)} %bitcast.14), slice={[0:15], [120:128]} | slice | bytes 960 | tf_op jit(solution)/shard_map/slice | solution.py:336
  2.1 0.8 %fusion = s32[136,16]{0,1:T(8,128)S(1)} fusion(s32[15,8]{1,0:T(8,128)S(1)} %slice.4, s32[16,128]{1,0:T(8,128)} %bitcast.15), kind=kLoop, calls=%fused_computation.1 | loop fusion | flops 6528 | bytes 17376 | tf_op jit(solution)/shard_map/transpose | solution.py:341
  2.9 0.0 copy-done
  2.9 0.6 %copy.19.taps_ref = f32[7,3,256]{2,1,0:T(4,128)} copy(f32[7,3,256]{2,0,1:T(8,128)S(1)} %constant_dynamic-slice_fusion) | data formatting | bytes 43008
  3.5 1.3 %dynamic-slice_bitcast_fusion = (f32[16,256]{1,0:T(8,128)}, f32[16,256]{1,0:T(8,128)}) fusion(f32[4096,16]{0,1:T(8,128)} %param.9, s32[]{:T(128)S(6)} %select_n.2, f32[4096,16]{0,1:T(8,128)} %param.10), kind=kLoop, calls=%fused_computation.3 | loop fusion | bytes 65540 | tf_op jit(solution)/shard_map/transpose | solution.py:347
  4.9 0.1 copy.13
  5.0 1.4 %copy.14 = bf16[512,3,256]{0,2,1:T(8,128)(2,1)S(1)} copy(bf16[512,3,256]{2,0,1:T(8,128)(2,1)} %param.7) | data formatting | bytes 1572864 | tf_op args[1]
  6.4 0.1 copy.15
  6.5 1.2 %copy.18.tab_ref = bf16[512,768]{1,0:T(8,128)(2,1)} copy(bf16[512,768]{0,1:T(8,128)(2,1)S(1)} %bitcast.12) | data formatting | bytes 1572864 | tf_op jit(solution)/shard_map/reshape | solution.py:343
  7.6 1.6 %reshape.17.ids_ref = s32[2176,1]{1,0:T(8,128)} reshape(s32[136,16]{1,0:T(8,128)S(1)} %copy.13) | data formatting | bytes 17408 | tf_op jit(solution)/shard_map/reshape | solution.py:341
  9.2 36.0 %shard_map.64 = bf16[128,4096]{1,0:T(8,128)(2,1)} custom-call(s32[2176,1]{1,0:T(8,128)} %reshape.17.ids_ref, bf16[512,768]{1,0:T(8,128)(2,1)} %copy.18.tab_ref, f32[7,3,256]{2,1,0:T(4,128)} %copy.19.taps_ref, f32[16,256]{1,0:T(8,128)} %get-tuple-element.6.decay_ref, f32[16,256]{1,0:T(8,128)} %get-tuple-element.5.residue_ref, f32[1,256]{1,0:T(1,128)} %bitcast.16), custom_call_target="tpu_custom_call" | custom-call | tf_op jit(solution)/shard_map/pallas_call | solution.py:351
  45.2 2.3 %copy.21 = bf16[128,4096]{1,0:T(8,128)(2,1)} copy(bf16[128,4096]{1,0:T(8,128)(2,1)} %shard_map.64) | data formatting | bytes 2097152
  (1 shorter events, 0.0 us)
Async XLA Ops:
  0.0 2.9 %copy-start = (f32[7,3,4096]{2,0,1:T(8,128)S(1)}, f32[7,3,4096]{2,0,1:T(8,128)}, u32[]{:S(2)}) copy-start(f32[7,3,4096]{2,0,1:T(8,128)} %param.8) | copy-start | bytes 1032196

commit v2 on v1

--- a/solution.py
+++ b/solution.py
@@ -151,12 +151,18 @@
     width,
     modes,
     ids_ref,
+    all_tab_ref,
+    all_taps_ref,
+    all_decay_ref,
+    all_residue_ref,
+    all_skip_ref,
+    out_ref,
     tab_ref,
     taps_ref,
     decay_ref,
     residue_ref,
     skip_ref,
-    out_ref,
+    load_sem,
     hot_ref,
     x_ref,
     query_ref,
@@ -176,9 +182,23 @@
     slots = pieces // SUB
     parts = half // SUB
     share = skip_ref.shape[1]
-    vocab = tab_ref.shape[0]
+    vocab = tab_ref.shape[1]
     blocks = share // LANES
     length = pieces * local
+    mine = pl.ds(pl.multiple_of(me * share, LANES), share)
+    loads = (
+        (all_tab_ref, tab_ref),
+        (all_taps_ref.at[:, :, mine], taps_ref),
+        (all_decay_ref.at[:, mine], decay_ref),
+        (all_residue_ref.at[:, mine], residue_ref),
+        (all_skip_ref.at[:, mine], skip_ref),
+    )
+    loads = [
+        pltpu.make_async_copy(source, target, load_sem.at[i])
+        for i, (source, target) in enumerate(loads)
+    ]
+    for load in loads:
+        load.start()
     barrier = pltpu.get_barrier_semaphore()
     for step in range(1, pieces):
         peer = lax.rem(me + step, pieces)
@@ -186,10 +206,18 @@
 
     rows = (HALO + local) * pieces
     cut = rows // 4
-    for i in range(4):
-        span = pl.ds(i * cut, cut)
-        entry = lax.broadcasted_iota(jnp.int32, (cut, vocab), 1)
-        hot_ref[span, :] = jnp.where(ids_ref[span, :] == entry, 1.0, 0.0).astype(jnp.bfloat16)
+    ids = ids_ref[...]
+    before = jnp.where(
+        lax.broadcasted_iota(jnp.int32, ids.shape, 0) == 0, -1, pltpu.roll(ids, 1, axis=0)
+    )
+    entry = lax.broadcasted_iota(jnp.int32, (pieces, vocab), 1)
+    for t in range(-HALO, local):
+        column = ids[:, t : t + 1] if t >= 0 else before[:, local + t : local + t + 1]
+        hot_ref[(HALO + t) * pieces : (HALO + t + 1) * pieces, :] = jnp.where(
+            column == entry, 1.0, 0.0
+        ).astype(jnp.bfloat16)
+    for load in loads:
+        load.wait()
 
     def remote(block, peer, source):
         column = pl.ds(pl.multiple_of(source * share + block * LANES, LANES), LANES)
@@ -214,7 +242,7 @@
         coef_ref[0] = pole
         coef_ref[1] = residue_ref[:, lane] * jnp.sqrt(2.0 * rate)
         skip = wide(skip_ref[:, lane])
-        table = tab_ref[:, block * 3 * LANES : (block + 1) * 3 * LANES]
+        table = jnp.concatenate([tab_ref[j, :, lane] for j in range(3)], axis=1)
         for i in range(4):
             span = pl.ds(i * cut, cut)
             x_ref[span, :] = jnp.dot(hot_ref[span, :], table, preferred_element_type=jnp.float32)
@@ -223,7 +251,7 @@
             base = pl.multiple_of(slot * SUB, SUB)
             poles = [wide(coef_ref[0, s : s + 1, :]) for s in range(modes)]
             taps = [
-                [wide(taps_ref[lag, j : j + 1, lane]) for lag in range(width)] for j in range(3)
+                [wide(taps_ref[j, lag : lag + 1, lane]) for lag in range(width)] for j in range(3)
             ]
 
             def step(i, state):
@@ -324,36 +352,29 @@
 
 def scan_body(token_ids, vocab_table, short_filter, residue, decay, skip_gain):
     pieces = lax.axis_size("seq")
-    place = lax.axis_index("seq")
     length = token_ids.shape[0]
     local = length // pieces
     vocab, streams, share = vocab_table.shape
     width = short_filter.shape[0]
     modes = decay.shape[1]
     blocks = share // LANES
-    spread = jnp.concatenate(
-        [
-            jnp.concatenate([jnp.full((1, HALO), -1, jnp.int32), token_ids.reshape(pieces, local)[:-1, local - HALO :]]),
-            token_ids.reshape(pieces, local),
-        ],
-        axis=1,
-    )
-    ids = spread.T.reshape((HALO + local) * pieces, 1)
-    table = vocab_table.reshape(vocab, streams, blocks, LANES).transpose(0, 2, 1, 3)
-    table = table.reshape(vocab, streams * share)
-    start = place * share
-    taps = lax.dynamic_slice_in_dim(short_filter, start, share, 2)
-    chan_decay = lax.dynamic_slice_in_dim(decay, start, share, 0).T
-    chan_residue = lax.dynamic_slice_in_dim(residue, start, share, 0).T
-    skip = lax.dynamic_slice_in_dim(skip_gain, start, share, 0)[None]
+    ids = token_ids.reshape(pieces, local)
+    table = vocab_table.transpose(1, 0, 2)
+    taps = short_filter.transpose(1, 0, 2)
     rows = (HALO + local) * pieces
     vmem = pl.BlockSpec(memory_space=pltpu.VMEM)
     return pl.pallas_call(
         functools.partial(scan_kernel, pieces, local, width, modes),
-        out_shape=jax.ShapeDtypeStruct((local, pieces * share), jnp.bfloat16),
-        in_specs=[vmem] * 6,
-        out_specs=pl.BlockSpec(memory_space=pl.ANY),
+        out_shape=pltpu.VMEM((local, pieces * share), jnp.bfloat16),
+        in_specs=[vmem] + [pl.BlockSpec(memory_space=pl.ANY)] * 5,
+        out_specs=pl.BlockSpec(memory_space=pltpu.VMEM),
         scratch_shapes=[
+            pltpu.VMEM((streams, vocab, share), vocab_table.dtype),
+            pltpu.VMEM((streams, width, share), jnp.float32),
+            pltpu.VMEM((modes, share), jnp.float32),
+            pltpu.VMEM((modes, share), jnp.float32),
+            pltpu.VMEM((1, share), jnp.float32),
+            pltpu.SemaphoreType.DMA((5,)),
             pltpu.VMEM((rows, vocab), jnp.bfloat16),
             pltpu.VMEM((rows, streams * LANES), jnp.float32),
             pltpu.VMEM((length, LANES), jnp.float32),
@@ -368,7 +389,7 @@
             pltpu.SemaphoreType.DMA((blocks,)),
         ],
         compiler_params=pltpu.CompilerParams(collective_id=0, has_side_effects=True),
-    )(ids, table, taps, chan_decay, chan_residue, skip)
+    )(ids, table, taps, decay.T, residue.T, skip_gain[None])
 
 
 def fits(mesh, share, local, width):

time: 47.9 us -> 37.2 us (0.78)
  local copies, waits for them, and re-layouts: 10.7 us -> 0.97 us
  other arithmetic: 0.77 us -> 0 us
    unnamed x5 -> x1, local copies, waits for them, and re-layouts: 4.32 us -> 0.97 us
    reshape x2 -> x0, local copies, waits for them, and re-layouts: 2.77 us -> none  [the longest x1 1.61 us: scan_body(): ids = spread.T.reshape((HALO + local) * pieces, 1)]
    transpose x3 -> x0, local copies, waits for them, and re-layouts: 1.51 us -> none  [the longest x1 1.34 us: scan_body(): chan_residue = lax.dynamic_slice_in_dim(residue, start, share, 0).T]
    dynamic_slice x2 -> x0, local copies, waits for them, and re-layouts: 1.38 us -> none  [the longest x1 1.37 us: scan_body(): skip = lax.dynamic_slice_in_dim(skip_gain, start, share, 0)[None]]
    transpose x1 -> x0, other arithmetic: 0.77 us -> none  [scan_body(): ids = spread.T.reshape((HALO + local) * pieces, 1)]
    slice x1 -> x0, local copies, waits for them, and re-layouts: 0.77 us -> none  [scan_body(): token_ids.reshape(pieces, local)[:-1, local - HALO:]]
where the time goes in v2:
time: 37.2 us; the launch traced here: 37 us
  Pallas kernels  36 us (97%)
  local copies, waits for them, and re-layouts  0.97 us (3%)
    pallas_call x1, Pallas kernels, scan_body(): pl.pallas_call(functools.partial(scan_kernel, pieces, local, width, modes...  36 us
    unnamed x1, local copies, waits for them, and re-layouts  0.97 us

profile of v2, /device:TPU:0, one launch (start us, length us, event | category | flops | bytes accessed | tf_op | source)
XLA Modules:
  0.0 37.0 jit_solution(9375065644760433725)
XLA Ops:
  0.0 36.0 %shard_map.64 = bf16[128,4096]{1,0:T(8,128)(2,1)S(1)} custom-call(s32[16,128]{1,0:T(8,128)} %bitcast.11, bf16[3,512,256]{2,1,0:T(8,128)(2,1)} %bitcast.6, f32[3,7,4096]{2,1,0:T(8,128)} %bitcast.7, f32[16,4096]{1,0:T(8,128)} %bitcast.8, f32[16,4096]{1,0:T(8,128)} %bitcast.9, f32[1,4096]{1,0:T(1,128)} %bitcast.10), custom_call_target="tpu_custom_call" | custom-call | tf_op jit(solution)/shard_map/pallas_call | solution.py:366
  36.0 1.0 %copy.8 = bf16[128,4096]{1,0:T(8,128)(2,1)} copy(bf16[128,4096]{1,0:T(8,128)(2,1)S(1)} %shard_map.64) | data formatting | bytes 2097152

commit v3 on v2

--- a/solution.py
+++ b/solution.py
@@ -138,11 +138,21 @@
 SUB = 8
 HALO = 8
 UNROLL = 8
+CUTS = 4
+SPLITS = 2
 MESH = pl.DeviceIdType.MESH
 
 
 def wide(row):
     return jnp.broadcast_to(row, (SUB, LANES))
+
+
+def flip(value, mask, limit):
+    result, bit = 0, 1
+    while bit < limit:
+        result = result + bit * ((value // bit + mask // bit) % 2)
+        bit = 2 * bit
+    return result
 
 
 def scan_kernel(
@@ -177,10 +187,7 @@
     own_sem,
 ):
     me = lax.axis_index("seq")
-    half = pieces // 2
-    near = me // half
     slots = pieces // SUB
-    parts = half // SUB
     share = skip_ref.shape[1]
     vocab = tab_ref.shape[1]
     blocks = share // LANES
@@ -204,35 +211,49 @@
         peer = lax.rem(me + step, pieces)
         pl.semaphore_signal(barrier, inc=1, device_id={"seq": peer}, device_id_type=MESH)
 
-    rows = (HALO + local) * pieces
-    cut = rows // 4
+    cut = (HALO + local) * pieces // CUTS
     ids = ids_ref[...]
     before = jnp.where(
         lax.broadcasted_iota(jnp.int32, ids.shape, 0) == 0, -1, pltpu.roll(ids, 1, axis=0)
     )
     entry = lax.broadcasted_iota(jnp.int32, (pieces, vocab), 1)
-    for t in range(-HALO, local):
-        column = ids[:, t : t + 1] if t >= 0 else before[:, local + t : local + t + 1]
-        hot_ref[(HALO + t) * pieces : (HALO + t + 1) * pieces, :] = jnp.where(
-            column == entry, 1.0, 0.0
-        ).astype(jnp.bfloat16)
+    count = (HALO + local) // CUTS
+
+    def build(i):
+        for t in range(i * count - HALO, (i + 1) * count - HALO):
+            column = ids[:, t : t + 1] if t >= 0 else before[:, local + t : local + t + 1]
+            hot_ref[(HALO + t) * pieces : (HALO + t + 1) * pieces, :] = jnp.where(
+                column == entry, 1.0, 0.0
+            ).astype(jnp.bfloat16)
+
+    build(0)
     for load in loads:
         load.wait()
 
-    def remote(block, peer, source):
-        column = pl.ds(pl.multiple_of(source * share + block * LANES, LANES), LANES)
+    height = local // SPLITS
+
+    def place(block, part, source):
+        return out_ref.at[
+            pl.ds(part * height, height),
+            pl.ds(pl.multiple_of(source * share + block * LANES, LANES), LANES),
+        ]
+
+    def remote(block, part, peer, source):
         return pltpu.make_async_remote_copy(
-            src_ref=send_ref.at[block, peer],
-            dst_ref=out_ref.at[:, column],
-            send_sem=send_sem.at[block, peer],
-            recv_sem=recv_sem.at[block, source],
+            src_ref=send_ref.at[block, peer, pl.ds(part * height, height)],
+            dst_ref=place(block, part, source),
+            send_sem=send_sem.at[block, part, peer],
+            recv_sem=recv_sem.at[block, part, source],
             device_id={"seq": peer},
             device_id_type=MESH,
         )
 
-    def own(block):
-        column = pl.ds(pl.multiple_of(me * share + block * LANES, LANES), LANES)
-        return pltpu.make_async_copy(send_ref.at[block, me], out_ref.at[:, column], own_sem.at[block])
+    def own(block, part):
+        return pltpu.make_async_copy(
+            send_ref.at[block, me, pl.ds(part * height, height)],
+            place(block, part, me),
+            own_sem.at[block, part],
+        )
 
     for block in range(blocks):
         lane = pl.ds(block * LANES, LANES)
@@ -243,7 +264,9 @@
         coef_ref[1] = residue_ref[:, lane] * jnp.sqrt(2.0 * rate)
         skip = wide(skip_ref[:, lane])
         table = jnp.concatenate([tab_ref[j, :, lane] for j in range(3)], axis=1)
-        for i in range(4):
+        for i in range(CUTS):
+            if block == 0 and i + 1 < CUTS:
+                build(i + 1)
             span = pl.ds(i * cut, cut)
             x_ref[span, :] = jnp.dot(hot_ref[span, :], table, preferred_element_type=jnp.float32)
 
@@ -290,64 +313,57 @@
             begin_ref[pl.ds(k, modes, stride=pieces), :] = carry
             carry = leap * carry + end_ref[pl.ds(k, modes, stride=pieces), :]
 
-        for side in range(2):
-            group = near if side else 1 - near
-            for part in range(parts):
-                first = group * half + part * SUB
-                base = pl.multiple_of(first, SUB)
-                poles = [wide(coef_ref[0, s : s + 1, :]) for s in range(modes)]
-                coefs = [wide(coef_ref[1, s : s + 1, :]) for s in range(modes)]
-
-                def step(i, state):
-                    state = list(state)
-                    for t in range(UNROLL):
-                        at = pl.multiple_of((i * UNROLL + t) * pieces + base, SUB)
-                        gated = gated_ref[pl.ds(at, SUB), :]
-                        terms = [skip * gated]
-                        for s in range(modes):
-                            state[s] = poles[s] * state[s] + gated
-                            terms.append(coefs[s] * state[s])
-                            if len(terms) == 5:
-                                terms = [((terms[0] + terms[1]) + (terms[2] + terms[3])) + terms[4]]
-                        total = terms[0]
-                        for term in terms[1:]:
-                            total = total + term
-                        turn_ref[pl.ds(pl.multiple_of((i * UNROLL + t) * SUB, SUB), SUB), :] = (
-                            query_ref[pl.ds(at, SUB), :] * total
-                        )
-                    return tuple(state)
-
-                state = tuple(
-                    begin_ref[pl.ds(pl.multiple_of(s * pieces + base, SUB), SUB), :]
-                    for s in range(modes)
-                )
-                lax.fori_loop(0, local // UNROLL, step, state)
+        for far in range(slots - 1, -1, -1):
+            first = flip(me // SUB, far, slots) * SUB
+            base = pl.multiple_of(first, SUB)
+            poles = [wide(coef_ref[0, s : s + 1, :]) for s in range(modes)]
+            coefs = [wide(coef_ref[1, s : s + 1, :]) for s in range(modes)]
+
+            def step(i, state):
+                state = list(state)
+                for t in range(UNROLL):
+                    at = pl.multiple_of((i * UNROLL + t) * pieces + base, SUB)
+                    gated = gated_ref[pl.ds(at, SUB), :]
+                    terms = [skip * gated]
+                    for s in range(modes):
+                        state[s] = poles[s] * state[s] + gated
+                        terms.append(coefs[s] * state[s])
+                        if len(terms) == 5:
+                            terms = [((terms[0] + terms[1]) + (terms[2] + terms[3])) + terms[4]]
+                    total = terms[0]
+                    for term in terms[1:]:
+                        total = total + term
+                    turn_ref[pl.ds(pl.multiple_of((i * UNROLL + t) * SUB, SUB), SUB), :] = (
+                        query_ref[pl.ds(at, SUB), :] * total
+                    )
+                return tuple(state)
+
+            state = tuple(
+                begin_ref[pl.ds(pl.multiple_of(s * pieces + base, SUB), SUB), :]
+                for s in range(modes)
+            )
+            for part in range(SPLITS):
+                low = part * height
+                state = lax.fori_loop(low // UNROLL, (low + height) // UNROLL, step, state)
                 for k in range(SUB):
-                    send_ref[block, first + k] = turn_ref[pl.ds(k, local, stride=SUB), :].astype(
-                        jnp.bfloat16
-                    )
-                if block == 0 and side == 0 and part == 0:
+                    send_ref[block, first + k, low : low + height, :] = turn_ref[
+                        pl.ds(low * SUB + k, height, stride=SUB), :
+                    ].astype(jnp.bfloat16)
+                if block == 0 and far == slots - 1 and part == 0:
                     pl.semaphore_wait(barrier, pieces - 1)
                 for k in range(SUB):
-                    peer = first + lax.rem(me + k, SUB)
-                    if side == 0:
-                        remote(block, peer, me).start()
+                    if far == 0 and k == 0:
+                        own(block, part).start()
                     else:
-
-                        @pl.when(peer != me)
-                        def _():
-                            remote(block, peer, me).start()
-
-                        @pl.when(peer == me)
-                        def _():
-                            own(block).start()
+                        remote(block, part, flip(me, far * SUB + k, pieces), me).start()
 
     for block in range(blocks):
-        own(block).wait()
-        for step in range(1, pieces):
-            remote(block, lax.rem(me + step, pieces), me).wait_send()
-        for step in range(1, pieces):
-            remote(block, me, lax.rem(me + step, pieces)).wait_recv()
+        for part in range(SPLITS):
+            own(block, part).wait()
+            for step in range(1, pieces):
+                remote(block, part, flip(me, step, pieces), me).wait_send()
+            for step in range(1, pieces):
+                remote(block, part, me, flip(me, step, pieces)).wait_recv()
 
 
 def scan_body(token_ids, vocab_table, short_filter, residue, decay, skip_gain):
@@ -384,9 +400,9 @@
             pltpu.VMEM((2, modes, LANES), jnp.float32),
             pltpu.VMEM((local * SUB, LANES), jnp.float32),
             pltpu.VMEM((blocks, pieces, local, LANES), jnp.bfloat16),
-            pltpu.SemaphoreType.DMA((blocks, pieces)),
-            pltpu.SemaphoreType.DMA((blocks, pieces)),
-            pltpu.SemaphoreType.DMA((blocks,)),
+            pltpu.SemaphoreType.DMA((blocks, SPLITS, pieces)),
+            pltpu.SemaphoreType.DMA((blocks, SPLITS, pieces)),
+            pltpu.SemaphoreType.DMA((blocks, SPLITS)),
         ],
         compiler_params=pltpu.CompilerParams(collective_id=0, has_side_effects=True),
     )(ids, table, taps, decay.T, residue.T, skip_gain[None])
@@ -394,7 +410,8 @@
 
 def fits(mesh, share, local, width):
     pieces = mesh.shape["seq"]
-    return share % LANES == 0 and pieces % (2 * SUB) == 0 and local % 16 == 0 and width <= HALO + 1
+    even = pieces % (2 * SUB) == 0 and pieces & (pieces - 1) == 0
+    return share % LANES == 0 and even and local % (16 * SPLITS) == 0 and width <= HALO + 1
 
 
 def solution(mesh):

time: 37.2 us -> 36.6 us (0.984)
  Pallas kernels: 36 us -> 35.4 us
    pallas_call x1, Pallas kernels: 36 us -> 35.4 us  [scan_body(): pl.pallas_call(functools.partial(scan_kernel, pieces, local, width, modes...]
where the time goes in v3:
time: 36.6 us; the launch traced here: 36.4 us
  Pallas kernels  35.4 us (97%)
  local copies, waits for them, and re-layouts  0.97 us (3%)
    pallas_call x1, Pallas kernels, scan_body(): pl.pallas_call(functools.partial(scan_kernel, pieces, local, width, modes...  35.4 us
    unnamed x1, local copies, waits for them, and re-layouts  0.97 us

profile of v3, /device:TPU:0, one launch (start us, length us, event | category | flops | bytes accessed | tf_op | source)
XLA Modules:
  0.0 36.4 jit_solution(14704440391126807680)
XLA Ops:
  0.0 35.4 %shard_map.64 = bf16[128,4096]{1,0:T(8,128)(2,1)S(1)} custom-call(s32[16,128]{1,0:T(8,128)} %bitcast.11, bf16[3,512,256]{2,1,0:T(8,128)(2,1)} %bitcast.6, f32[3,7,4096]{2,1,0:T(8,128)} %bitcast.7, f32[16,4096]{1,0:T(8,128)} %bitcast.8, f32[16,4096]{1,0:T(8,128)} %bitcast.9, f32[1,4096]{1,0:T(1,128)} %bitcast.10), custom_call_target="tpu_custom_call" | custom-call | tf_op jit(solution)/shard_map/pallas_call | solution.py:382
  35.4 1.0 %copy.8 = bf16[128,4096]{1,0:T(8,128)(2,1)} copy(bf16[128,4096]{1,0:T(8,128)(2,1)S(1)} %shard_map.64) | data formatting | bytes 2097152

commit v4 on v3

--- a/solution.py
+++ b/solution.py
@@ -139,7 +139,7 @@
 HALO = 8
 UNROLL = 8
 CUTS = 4
-SPLITS = 2
+SPLITS = 1
 MESH = pl.DeviceIdType.MESH
 
 
@@ -147,12 +147,19 @@
     return jnp.broadcast_to(row, (SUB, LANES))
 
 
-def flip(value, mask, limit):
-    result, bit = 0, 1
+def toggles(value, limit):
+    steps, bit = [], 1
     while bit < limit:
-        result = result + bit * ((value // bit + mask // bit) % 2)
+        steps.append((bit, bit - 2 * bit * (value // bit % 2)))
         bit = 2 * bit
-    return result
+    return steps
+
+
+def flip(value, steps, mask):
+    for bit, step in steps:
+        if mask & bit:
+            value = value + step
+    return value
 
 
 def scan_kernel(
@@ -188,6 +195,7 @@
 ):
     me = lax.axis_index("seq")
     slots = pieces // SUB
+    steps = toggles(me, pieces)
     share = skip_ref.shape[1]
     vocab = tab_ref.shape[1]
     blocks = share // LANES
@@ -207,8 +215,8 @@
     for load in loads:
         load.start()
     barrier = pltpu.get_barrier_semaphore()
-    for step in range(1, pieces):
-        peer = lax.rem(me + step, pieces)
+    for mask in range(1, pieces):
+        peer = flip(me, steps, mask)
         pl.semaphore_signal(barrier, inc=1, device_id={"seq": peer}, device_id_type=MESH)
 
     cut = (HALO + local) * pieces // CUTS
@@ -238,12 +246,12 @@
             pl.ds(pl.multiple_of(source * share + block * LANES, LANES), LANES),
         ]
 
-    def remote(block, part, peer, source):
+    def remote(block, part, mask, peer, source):
         return pltpu.make_async_remote_copy(
             src_ref=send_ref.at[block, peer, pl.ds(part * height, height)],
             dst_ref=place(block, part, source),
-            send_sem=send_sem.at[block, part, peer],
-            recv_sem=recv_sem.at[block, part, source],
+            send_sem=send_sem.at[block, part, mask],
+            recv_sem=recv_sem.at[block, part, mask],
             device_id={"seq": peer},
             device_id_type=MESH,
         )
@@ -314,7 +322,7 @@
             carry = leap * carry + end_ref[pl.ds(k, modes, stride=pieces), :]
 
         for far in range(slots - 1, -1, -1):
-            first = flip(me // SUB, far, slots) * SUB
+            first = flip(me // SUB * SUB, steps, far * SUB)
             base = pl.multiple_of(first, SUB)
             poles = [wide(coef_ref[0, s : s + 1, :]) for s in range(modes)]
             coefs = [wide(coef_ref[1, s : s + 1, :]) for s in range(modes)]
@@ -355,15 +363,16 @@
                     if far == 0 and k == 0:
                         own(block, part).start()
                     else:
-                        remote(block, part, flip(me, far * SUB + k, pieces), me).start()
+                        mask = far * SUB + k
+                        remote(block, part, mask, flip(me, steps, mask), me).start()
 
     for block in range(blocks):
         for part in range(SPLITS):
             own(block, part).wait()
-            for step in range(1, pieces):
-                remote(block, part, flip(me, step, pieces), me).wait_send()
-            for step in range(1, pieces):
-                remote(block, part, me, flip(me, step, pieces)).wait_recv()
+            for mask in range(1, pieces):
+                peer = flip(me, steps, mask)
+                remote(block, part, mask, peer, me).wait_send()
+                remote(block, part, mask, me, peer).wait_recv()
 
 
 def scan_body(token_ids, vocab_table, short_filter, residue, decay, skip_gain):

time: 36.6 us -> 35 us (0.956)
  Pallas kernels: 35.4 us -> 33.7 us
    pallas_call x1, Pallas kernels: 35.4 us -> 33.7 us  [scan_body(): pl.pallas_call(functools.partial(scan_kernel, pieces, local, width, modes...]
where the time goes in v4:
time: 35 us; the launch traced here: 34.7 us
  Pallas kernels  33.7 us (96%)
  local copies, waits for them, and re-layouts  0.97 us (3%)
    pallas_call x1, Pallas kernels, scan_body(): pl.pallas_call(functools.partial(scan_kernel, pieces, local, width, modes...  33.7 us
    unnamed x1, local copies, waits for them, and re-layouts  0.97 us

profile of v4, /device:TPU:0, one launch (start us, length us, event | category | flops | bytes accessed | tf_op | source)
XLA Modules:
  0.0 34.7 jit_solution(14743482543433842465)
XLA Ops:
  0.0 33.7 %shard_map.64 = bf16[128,4096]{1,0:T(8,128)(2,1)S(1)} custom-call(s32[16,128]{1,0:T(8,128)} %bitcast.11, bf16[3,512,256]{2,1,0:T(8,128)(2,1)} %bitcast.6, f32[3,7,4096]{2,1,0:T(8,128)} %bitcast.7, f32[16,4096]{1,0:T(8,128)} %bitcast.8, f32[16,4096]{1,0:T(8,128)} %bitcast.9, f32[1,4096]{1,0:T(1,128)} %bitcast.10), custom_call_target="tpu_custom_call" | custom-call | tf_op jit(solution)/shard_map/pallas_call | solution.py:391
  33.7 1.0 %copy.8 = bf16[128,4096]{1,0:T(8,128)(2,1)} copy(bf16[128,4096]{1,0:T(8,128)(2,1)S(1)} %shard_map.64) | data formatting | bytes 2097152
